TPU v7x, 256 devices: a whole 4x4x8 slice. The times are simulated.
256 devices in a mesh: ctx: 16 (over z, core), row: 4 (over y), col: 4 (over x).
Axes of the slice: x: 4, y: 4, z: 8, core: 2. Of those that a mesh axis runs over, the one named last changes fastest.
Arguments:
- output_grad: bfloat16 [8192, 8192], P('ctx', ('row', 'col')), may hold values from -6 to 6
- conv_out: bfloat16 [8192, 8192], P('ctx', ('row', 'col')), may hold values from -9 to 9
- input_mix: bfloat16 [8192, 4, 256], P('ctx'), may hold values from -0.15625 to 0.15625
- output_mix: bfloat16 [8192, 4, 256], P('ctx'), may hold values from -1 to 1
- step_size: float32 [128, 8192], P(('row', 'col'), 'ctx'), may hold values from 0.5 to 2
- log_decay: float32 [128, 8192], P(('row', 'col'), 'ctx'), may hold values from -2.1 to 0, as said below
- skip_gain: float32 [128], P(('row', 'col')), may hold values from 0.5 to 2
- conv_weight: float32 [4, 8192], P(None, ('row', 'col')), may hold values from -3 to 3
- later_grad: float32 [128, 64, 256], P(('row', 'col')), may hold values from -32 to 32
- proj_weight: bfloat16 [8192, 8192], P('col', 'row'), may hold values from -0.0625 to 0.0625
Outputs:
- hidden_grad: bfloat16 [8192, 8192], P('ctx', ('col', 'row'))
- x_grad: bfloat16 [8192, 8192], P('ctx', ('row', 'col'))
- state_grad: float32 [16, 128, 64, 256], P('ctx', ('row', 'col'))
Inputs may be any that keep to these rules, and one draw needn't show every extreme that they name: `log_decay`: the forward pass's log decay of each head at each token.
All inputs are finite; a program needn't handle non-finite values.
Results may differ from a plain program's by a relative error of at most 0.022.
Values may be sent and summed in bfloat16 or wider, within the bound.
No kernel may reach another device: no remote copies, remote signals or barrier semaphores. Data moves between devices by JAX's collectives and lax.ppermute only.
A program may use at most 128 MiB of HBM per device.

v0:
```python
import jax
import jax.numpy as jnp
from jax import lax
from jax.sharding import PartitionSpec as P

HD = 64
HPG = 32
KW = 4


def from_behind(value, axis, steps):
    count = lax.axis_size(axis)
    first, last = (max(0, -steps), min(count, count - steps))
    return lax.ppermute(value, axis, [(source, source + steps) for source in range(first, last)])


def on_device(
    output_grad,
    conv_out,
    input_mix,
    output_mix,
    step_size,
    log_decay,
    skip_gain,
    conv_weight,
    later_grad,
    proj_weight,
):
    tokens_dev = output_grad.shape[0]
    heads_dev = step_size.shape[0]
    head_block = lax.axis_index("row") * lax.axis_size("col") + lax.axis_index("col")
    group = head_block * heads_dev // HPG
    write_rows = lax.dynamic_index_in_dim(input_mix, group, 1, keepdims=False)
    read_rows = lax.dynamic_index_in_dim(output_mix, group, 1, keepdims=False)
    cumulative = jnp.cumsum(log_decay, axis=1)
    block_end = cumulative[:, -1]
    decays = jnp.exp(block_end)
    per_head = output_grad.reshape(tokens_dev, heads_dev, HD)
    weighted = (jnp.exp(cumulative).T[:, :, None] * per_head.astype(jnp.float32)).astype(
        jnp.bfloat16
    )
    block_sum = jnp.einsum("shd,sn->hdn", weighted, read_rows, preferred_element_type=jnp.float32)
    is_last = lax.axis_index("ctx") == lax.axis_size("ctx") - 1

    def chain_turn(turn_index, estimate):
        passed = from_behind(
            (block_sum + decays[:, None, None] * estimate).astype(jnp.bfloat16), "ctx", -1
        ).astype(jnp.float32)
        return jnp.where(is_last, later_grad, passed)

    carried = lax.fori_loop(
        0,
        lax.axis_size("ctx") - 1,
        chain_turn,
        jnp.where(is_last, later_grad, jnp.zeros_like(later_grad)),
    )
    state_start = block_sum + decays[:, None, None] * carried
    scores = jnp.dot(write_rows, read_rows.T, preferred_element_type=jnp.float32)
    positions = jnp.arange(tokens_dev)
    causal = positions[None, :] >= positions[:, None]
    offsets = cumulative[:, None, :] - cumulative[:, :, None]
    mixing = (jnp.exp(jnp.where(causal[None], offsets, -jnp.inf)) * scores[None]).astype(
        jnp.bfloat16
    )
    intra = jnp.einsum("hts,shd->thd", mixing, per_head, preferred_element_type=jnp.float32)
    inter = jnp.einsum(
        "hdn,tn->thd", carried, write_rows.astype(jnp.float32), precision=lax.Precision.HIGHEST
    )
    inter = inter * jnp.exp(block_end[:, None] - cumulative).T[:, :, None]
    input_grad = step_size.T[:, :, None] * (intra + inter) + skip_gain[
        None, :, None
    ] * per_head.astype(jnp.float32)
    flat_grad = input_grad.reshape(tokens_dev, heads_dev * HD)
    activated = conv_out.astype(jnp.float32)
    sigma = jax.nn.sigmoid(activated)
    pre_grad = (flat_grad * sigma * (1.0 + activated * (1.0 - sigma))).astype(jnp.bfloat16)
    rim_rows = from_behind(pre_grad[: KW - 1], "ctx", -1)
    extended = jnp.concatenate([pre_grad, rim_rows], axis=0).astype(jnp.float32)
    accum = jnp.zeros(pre_grad.shape, jnp.float32)
    for tap in range(KW):
        accum = accum + conv_weight[tap][None, :] * extended[tap : tap + tokens_dev]
    x_grad = accum.astype(jnp.bfloat16)
    partial_grad = lax.dot_general(
        lax.all_gather(x_grad, "col", axis=1, tiled=True),
        proj_weight,
        (((1,), (1,)), ((), ())),
        preferred_element_type=jnp.float32,
    )
    hidden_grad = lax.psum_scatter(
        partial_grad.astype(jnp.bfloat16), "row", scatter_dimension=1, tiled=True
    )
    return (hidden_grad, x_grad, state_start[None])


def solution(mesh):
    return jax.shard_map(
        on_device,
        mesh=mesh,
        in_specs=(
            P("ctx", ("row", "col")),
            P("ctx", ("row", "col")),
            P("ctx", None, None),
            P("ctx", None, None),
            P(("row", "col"), "ctx"),
            P(("row", "col"), "ctx"),
            P(("row", "col")),
            P(None, ("row", "col")),
            P(("row", "col"), None, None),
            P("col", "row"),
        ),
        out_specs=(
            P("ctx", ("col", "row")),
            P("ctx", ("row", "col")),
            P("ctx", ("row", "col"), None, None),
        ),
        check_vma=False,
    )
```

profile of v0, /device:TPU:1, one launch (start us, length us, event | category | flops | bytes accessed | tf_op | source)
XLA Modules:
  0.0 251.9 jit_solution(11634387616972478772)
XLA Ops:
  7.2 2.3 reduce-window.6
  11.5 2.6 %constant_dynamic-slice_fusion = (bf16[512,1,256]{2,1,0:T(2,128)(2,1)S(1)}, bf16[512,1,256]{2,1,0:T(2,128)(2,1)S(1)}) fusion(bf16[512,4,256]{2,1,0:T(4,128)(2,1)} %param.15, s32[]{:T(128)S(6)} %select_n.30, bf16[512,4,256]{2,1,0:T(4,128)(2,1)} %param.14), kind=kLoop, calls=%fused_computation.48 | loop fusion | bytes 1048580 | tf_op jit(solution)/shard_map/jit(dynamic_index_in_dim)/dynamic_slice | solution.py:34
  15.8 4.3 %fusion.2 = f32[512,8,64]{0,2,1:T(8,128)} fusion(bf16[512,8,64]{0,2,1:T(8,128)(2,1)S(1)} %bitcast.41, f32[512,512]{1,0:T(8,128)} %fusion.20, f32[8,512]{1,0:T(8,128)S(1)} %get-tuple-element.49, pred[512,512]{1,0:T(8,128)(4,1)S(1)} %iota_compare_fusion), kind=kOutput, calls=%fused_computation.6 | convolution fusion | flops 276824064 | bytes 2899968 | tf_op jit(solution)/shard_map/hts,shd->thd/dot_general | solution.py:65
  20.1 119.6 %while.10 = (s32[]{:T(128)}, f32[8,64,256]{2,1,0:T(8,128)S(1)}, pred[]{:T(512)}, f32[8]{0:T(128)S(1)}, f32[8,64,256]{2,1,0:T(8,128)S(1)}, /*index=5*/f32[8,64,256]{2,1,0:T(8,128)S(1)}, s32[]{:T(128)}) while((s32[]{:T(128)}, f32[8,64,256]{2,1,0:T(8,128)S(1)}, pred[]{:T(512)}, f32[8]{0:T(128)S(1)}, f32[8,64,256]{2,1,0:T(8,128)S(1)}, ...), condition=%wide.region_3.4_spmd, body=%wide.region_2.3_spmd.sunk | while | flops 655362 | bytes 3670166 | solution.py:51
  20.2 5.2 %collective-permute-start = (bf16[8,64,256]{2,1,0:T(8,128)(2,1)S(1)}, bf16[8,64,256]{2,1,0:T(8,128)(2,1)S(1)}, u32[]{:S(2)}, u32[]{:S(2)}) collective-permute-start(bf16[8,64,256]{2,1,0:T(8,128)(2,1)S(1)} %add_convert_fusion.2), channel_id=1, source_target_pairs={{16,0},{32,16},{48,32},{64,48},{80,64},{96,80},{112,96},{128,112},... | collective-permute-start | bytes 786440 | tf_op jit(solution)/shard_map/while/body/eval_jaxpr/ppermute | solution.py:14
  25.4 3.8 %collective-permute-done = bf16[8,64,256]{2,1,0:T(8,128)(2,1)S(1)} collective-permute-done((bf16[8,64,256]{2,1,0:T(8,128)(2,1)S(1)}, bf16[8,64,256]{2,1,0:T(8,128)(2,1)S(1)}, u32[]{:S(2)}, u32[]{:S(2)}) %collective-permute-start) | collective-permute-done | bytes 262176 | tf_op jit(solution)/shard_map/while/body/eval_jaxpr/ppermute | solution.py:14
  29.4 1.9 collective-permute-start
  31.3 5.8 %collective-permute-done = bf16[8,64,256]{2,1,0:T(8,128)(2,1)S(1)} collective-permute-done((bf16[8,64,256]{2,1,0:T(8,128)(2,1)S(1)}, bf16[8,64,256]{2,1,0:T(8,128)(2,1)S(1)}, u32[]{:S(2)}, u32[]{:S(2)}) %collective-permute-start) | collective-permute-done | bytes 262176 | tf_op jit(solution)/shard_map/while/body/eval_jaxpr/ppermute | solution.py:14
  37.3 1.9 collective-permute-start
  39.2 5.8 %collective-permute-done = bf16[8,64,256]{2,1,0:T(8,128)(2,1)S(1)} collective-permute-done((bf16[8,64,256]{2,1,0:T(8,128)(2,1)S(1)}, bf16[8,64,256]{2,1,0:T(8,128)(2,1)S(1)}, u32[]{:S(2)}, u32[]{:S(2)}) %collective-permute-start) | collective-permute-done | bytes 262176 | tf_op jit(solution)/shard_map/while/body/eval_jaxpr/ppermute | solution.py:14
  45.2 1.9 collective-permute-start
  47.1 5.8 %collective-permute-done = bf16[8,64,256]{2,1,0:T(8,128)(2,1)S(1)} collective-permute-done((bf16[8,64,256]{2,1,0:T(8,128)(2,1)S(1)}, bf16[8,64,256]{2,1,0:T(8,128)(2,1)S(1)}, u32[]{:S(2)}, u32[]{:S(2)}) %collective-permute-start) | collective-permute-done | bytes 262176 | tf_op jit(solution)/shard_map/while/body/eval_jaxpr/ppermute | solution.py:14
  55.0 5.8 %collective-permute-done = bf16[8,64,256]{2,1,0:T(8,128)(2,1)S(1)} collective-permute-done((bf16[8,64,256]{2,1,0:T(8,128)(2,1)S(1)}, bf16[8,64,256]{2,1,0:T(8,128)(2,1)S(1)}, u32[]{:S(2)}, u32[]{:S(2)}) %collective-permute-start) | collective-permute-done | bytes 262176 | tf_op jit(solution)/shard_map/while/body/eval_jaxpr/ppermute | solution.py:14
  62.9 5.8 %collective-permute-done = bf16[8,64,256]{2,1,0:T(8,128)(2,1)S(1)} collective-permute-done((bf16[8,64,256]{2,1,0:T(8,128)(2,1)S(1)}, bf16[8,64,256]{2,1,0:T(8,128)(2,1)S(1)}, u32[]{:S(2)}, u32[]{:S(2)}) %collective-permute-start) | collective-permute-done | bytes 262176 | tf_op jit(solution)/shard_map/while/body/eval_jaxpr/ppermute | solution.py:14
  68.8 1.9 collective-permute-start
  70.8 5.8 %collective-permute-done = bf16[8,64,256]{2,1,0:T(8,128)(2,1)S(1)} collective-permute-done((bf16[8,64,256]{2,1,0:T(8,128)(2,1)S(1)}, bf16[8,64,256]{2,1,0:T(8,128)(2,1)S(1)}, u32[]{:S(2)}, u32[]{:S(2)}) %collective-permute-start) | collective-permute-done | bytes 262176 | tf_op jit(solution)/shard_map/while/body/eval_jaxpr/ppermute | solution.py:14
  76.7 1.9 collective-permute-start
  78.6 5.8 %collective-permute-done = bf16[8,64,256]{2,1,0:T(8,128)(2,1)S(1)} collective-permute-done((bf16[8,64,256]{2,1,0:T(8,128)(2,1)S(1)}, bf16[8,64,256]{2,1,0:T(8,128)(2,1)S(1)}, u32[]{:S(2)}, u32[]{:S(2)}) %collective-permute-start) | collective-permute-done | bytes 262176 | tf_op jit(solution)/shard_map/while/body/eval_jaxpr/ppermute | solution.py:14
  84.6 1.9 collective-permute-start
  86.5 5.8 %collective-permute-done = bf16[8,64,256]{2,1,0:T(8,128)(2,1)S(1)} collective-permute-done((bf16[8,64,256]{2,1,0:T(8,128)(2,1)S(1)}, bf16[8,64,256]{2,1,0:T(8,128)(2,1)S(1)}, u32[]{:S(2)}, u32[]{:S(2)}) %collective-permute-start) | collective-permute-done | bytes 262176 | tf_op jit(solution)/shard_map/while/body/eval_jaxpr/ppermute | solution.py:14
  94.4 5.8 %collective-permute-done = bf16[8,64,256]{2,1,0:T(8,128)(2,1)S(1)} collective-permute-done((bf16[8,64,256]{2,1,0:T(8,128)(2,1)S(1)}, bf16[8,64,256]{2,1,0:T(8,128)(2,1)S(1)}, u32[]{:S(2)}, u32[]{:S(2)}) %collective-permute-start) | collective-permute-done | bytes 262176 | tf_op jit(solution)/shard_map/while/body/eval_jaxpr/ppermute | solution.py:14
  102.3 5.8 %collective-permute-done = bf16[8,64,256]{2,1,0:T(8,128)(2,1)S(1)} collective-permute-done((bf16[8,64,256]{2,1,0:T(8,128)(2,1)S(1)}, bf16[8,64,256]{2,1,0:T(8,128)(2,1)S(1)}, u32[]{:S(2)}, u32[]{:S(2)}) %collective-permute-start) | collective-permute-done | bytes 262176 | tf_op jit(solution)/shard_map/while/body/eval_jaxpr/ppermute | solution.py:14
  110.2 5.8 %collective-permute-done = bf16[8,64,256]{2,1,0:T(8,128)(2,1)S(1)} collective-permute-done((bf16[8,64,256]{2,1,0:T(8,128)(2,1)S(1)}, bf16[8,64,256]{2,1,0:T(8,128)(2,1)S(1)}, u32[]{:S(2)}, u32[]{:S(2)}) %collective-permute-start) | collective-permute-done | bytes 262176 | tf_op jit(solution)/shard_map/while/body/eval_jaxpr/ppermute | solution.py:14
  118.1 5.8 %collective-permute-done = bf16[8,64,256]{2,1,0:T(8,128)(2,1)S(1)} collective-permute-done((bf16[8,64,256]{2,1,0:T(8,128)(2,1)S(1)}, bf16[8,64,256]{2,1,0:T(8,128)(2,1)S(1)}, u32[]{:S(2)}, u32[]{:S(2)}) %collective-permute-start) | collective-permute-done | bytes 262176 | tf_op jit(solution)/shard_map/while/body/eval_jaxpr/ppermute | solution.py:14
  126.0 5.8 %collective-permute-done = bf16[8,64,256]{2,1,0:T(8,128)(2,1)S(1)} collective-permute-done((bf16[8,64,256]{2,1,0:T(8,128)(2,1)S(1)}, bf16[8,64,256]{2,1,0:T(8,128)(2,1)S(1)}, u32[]{:S(2)}, u32[]{:S(2)}) %collective-permute-start) | collective-permute-done | bytes 262176 | tf_op jit(solution)/shard_map/while/body/eval_jaxpr/ppermute | solution.py:14
  133.9 5.8 %collective-permute-done = bf16[8,64,256]{2,1,0:T(8,128)(2,1)S(1)} collective-permute-done((bf16[8,64,256]{2,1,0:T(8,128)(2,1)S(1)}, bf16[8,64,256]{2,1,0:T(8,128)(2,1)S(1)}, u32[]{:S(2)}, u32[]{:S(2)}) %collective-permute-start) | collective-permute-done | bytes 262176 | tf_op jit(solution)/shard_map/while/body/eval_jaxpr/ppermute | solution.py:14
  139.7 2.0 fusion.5
  143.5 1.9 collective-permute-start.1
  145.5 3.0 %collective-permute-done.1 = bf16[3,512]{1,0:T(4,128)(2,1)S(1)} collective-permute-done((bf16[3,512]{1,0:T(4,128)(2,1)S(1)}, bf16[3,512]{1,0:T(4,128)(2,1)S(1)}, u32[]{:S(2)}, u32[]{:S(2)}) %collective-permute-start.1) | collective-permute-done | bytes 3104 | tf_op jit(solution)/shard_map/ppermute | solution.py:14
  149.9 52.7 %all-gather.2.cloned.1.call-done = bf16[512,2048]{1,0:T(8,128)(2,1)} async-done(((bf16[512,512]{1,0:T(8,128)(2,1)}), bf16[512,2048]{1,0:T(8,128)(2,1)}) %all-gather.2.cloned.1.call-update) | async-done | bytes 2097168 | tf_op jit(solution)/shard_map/all_gather | solution.py:84
  202.6 9.9 %convolution_convert_fusion = bf16[512,2048]{1,0:T(8,128)(2,1)} fusion(bf16[512,2048]{1,0:T(8,128)(2,1)} %all-gather.2.cloned.1.call-done, bf16[2048,2048]{1,0:T(8,128)(2,1)} %param.21), kind=kOutput, calls=%fused_computation.5 | convolution fusion | flops 4296015872 | bytes 12582912 | tf_op jit(solution)/shard_map/dot_general | solution.py:83
  213.4 31.6 %reduce-scatter.2.cloned.1.call-done = bf16[512,512]{1,0:T(8,128)(2,1)} async-done(((bf16[512,2048]{1,0:T(8,128)(2,1)}), bf16[512,512]{1,0:T(8,128)(2,1)}) %reduce-scatter.2.cloned.1.call-update) | async-done | bytes 524304 | tf_op jit(solution)/shard_map/reduce_scatter | solution.py:89
  (70 shorter events, 25.8 us)
Async XLA Ops:
  7.2 8.6 %copy-start = (f32[8,64,256]{2,1,0:T(8,128)S(1)}, f32[8,64,256]{2,1,0:T(8,128)}, u32[]{:S(2)}) copy-start(f32[8,64,256]{2,1,0:T(8,128)} %param.20) | copy-start | bytes 1572868
  7.2 195.4 %all-gather.2.cloned.1.call-start = ((), (), s32[]{:S(2)}) async-start(), calls=%async_computation.1 | async-start | bytes 2621440 | tf_op jit(solution)/shard_map/all_gather | solution.py:84
  20.1 119.6 %copy-start.1 = (f32[8,512]{1,0:T(8,128)S(1)}, f32[8,512]{1,0:T(8,128)}, u32[]{:S(2)}) copy-start(f32[8,512]{1,0:T(8,128)} %param.16) | copy-start | bytes 49156
  20.1 119.6 %copy-start.3 = (f32[8]{0:T(128)S(1)}, f32[8]{0:T(128)}, u32[]{:S(2)}) copy-start(f32[8]{0:T(128)} %param.18) | copy-start | bytes 100
  20.2 9.0 %collective-permute-start = (bf16[8,64,256]{2,1,0:T(8,128)(2,1)S(1)}, bf16[8,64,256]{2,1,0:T(8,128)(2,1)S(1)}, u32[]{:S(2)}, u32[]{:S(2)}) collective-permute-start(bf16[8,64,256]{2,1,0:T(8,128)(2,1)S(1)} %add_convert_fusion.2), channel_id=1, source_target_pairs={{16,0},{32,16},{48,32},{64,48},{80,64},{96,80},{112,96},{128,112},... | collective-permute-start | bytes 786440 | tf_op jit(solution)/shard_map/while/body/eval_jaxpr/ppermute | solution.py:14
  29.4 7.7 %collective-permute-start = (bf16[8,64,256]{2,1,0:T(8,128)(2,1)S(1)}, bf16[8,64,256]{2,1,0:T(8,128)(2,1)S(1)}, u32[]{:S(2)}, u32[]{:S(2)}) collective-permute-start(bf16[8,64,256]{2,1,0:T(8,128)(2,1)S(1)} %add_convert_fusion.2), channel_id=1, source_target_pairs={{16,0},{32,16},{48,32},{64,48},{80,64},{96,80},{112,96},{128,112},... | collective-permute-start | bytes 786440 | tf_op jit(solution)/shard_map/while/body/eval_jaxpr/ppermute | solution.py:14
  37.3 7.7 %collective-permute-start = (bf16[8,64,256]{2,1,0:T(8,128)(2,1)S(1)}, bf16[8,64,256]{2,1,0:T(8,128)(2,1)S(1)}, u32[]{:S(2)}, u32[]{:S(2)}) collective-permute-start(bf16[8,64,256]{2,1,0:T(8,128)(2,1)S(1)} %add_convert_fusion.2), channel_id=1, source_target_pairs={{16,0},{32,16},{48,32},{64,48},{80,64},{96,80},{112,96},{128,112},... | collective-permute-start | bytes 786440 | tf_op jit(solution)/shard_map/while/body/eval_jaxpr/ppermute | solution.py:14
  45.2 7.7 %collective-permute-start = (bf16[8,64,256]{2,1,0:T(8,128)(2,1)S(1)}, bf16[8,64,256]{2,1,0:T(8,128)(2,1)S(1)}, u32[]{:S(2)}, u32[]{:S(2)}) collective-permute-start(bf16[8,64,256]{2,1,0:T(8,128)(2,1)S(1)} %add_convert_fusion.2), channel_id=1, source_target_pairs={{16,0},{32,16},{48,32},{64,48},{80,64},{96,80},{112,96},{128,112},... | collective-permute-start | bytes 786440 | tf_op jit(solution)/shard_map/while/body/eval_jaxpr/ppermute | solution.py:14
  53.1 7.7 %collective-permute-start = (bf16[8,64,256]{2,1,0:T(8,128)(2,1)S(1)}, bf16[8,64,256]{2,1,0:T(8,128)(2,1)S(1)}, u32[]{:S(2)}, u32[]{:S(2)}) collective-permute-start(bf16[8,64,256]{2,1,0:T(8,128)(2,1)S(1)} %add_convert_fusion.2), channel_id=1, source_target_pairs={{16,0},{32,16},{48,32},{64,48},{80,64},{96,80},{112,96},{128,112},... | collective-permute-start | bytes 786440 | tf_op jit(solution)/shard_map/while/body/eval_jaxpr/ppermute | solution.py:14
  60.9 7.7 %collective-permute-start = (bf16[8,64,256]{2,1,0:T(8,128)(2,1)S(1)}, bf16[8,64,256]{2,1,0:T(8,128)(2,1)S(1)}, u32[]{:S(2)}, u32[]{:S(2)}) collective-permute-start(bf16[8,64,256]{2,1,0:T(8,128)(2,1)S(1)} %add_convert_fusion.2), channel_id=1, source_target_pairs={{16,0},{32,16},{48,32},{64,48},{80,64},{96,80},{112,96},{128,112},... | collective-permute-start | bytes 786440 | tf_op jit(solution)/shard_map/while/body/eval_jaxpr/ppermute | solution.py:14
  68.8 7.7 %collective-permute-start = (bf16[8,64,256]{2,1,0:T(8,128)(2,1)S(1)}, bf16[8,64,256]{2,1,0:T(8,128)(2,1)S(1)}, u32[]{:S(2)}, u32[]{:S(2)}) collective-permute-start(bf16[8,64,256]{2,1,0:T(8,128)(2,1)S(1)} %add_convert_fusion.2), channel_id=1, source_target_pairs={{16,0},{32,16},{48,32},{64,48},{80,64},{96,80},{112,96},{128,112},... | collective-permute-start | bytes 786440 | tf_op jit(solution)/shard_map/while/body/eval_jaxpr/ppermute | solution.py:14
  76.7 7.7 %collective-permute-start = (bf16[8,64,256]{2,1,0:T(8,128)(2,1)S(1)}, bf16[8,64,256]{2,1,0:T(8,128)(2,1)S(1)}, u32[]{:S(2)}, u32[]{:S(2)}) collective-permute-start(bf16[8,64,256]{2,1,0:T(8,128)(2,1)S(1)} %add_convert_fusion.2), channel_id=1, source_target_pairs={{16,0},{32,16},{48,32},{64,48},{80,64},{96,80},{112,96},{128,112},... | collective-permute-start | bytes 786440 | tf_op jit(solution)/shard_map/while/body/eval_jaxpr/ppermute | solution.py:14
  84.6 7.7 %collective-permute-start = (bf16[8,64,256]{2,1,0:T(8,128)(2,1)S(1)}, bf16[8,64,256]{2,1,0:T(8,128)(2,1)S(1)}, u32[]{:S(2)}, u32[]{:S(2)}) collective-permute-start(bf16[8,64,256]{2,1,0:T(8,128)(2,1)S(1)} %add_convert_fusion.2), channel_id=1, source_target_pairs={{16,0},{32,16},{48,32},{64,48},{80,64},{96,80},{112,96},{128,112},... | collective-permute-start | bytes 786440 | tf_op jit(solution)/shard_map/while/body/eval_jaxpr/ppermute | solution.py:14
  92.5 7.7 %collective-permute-start = (bf16[8,64,256]{2,1,0:T(8,128)(2,1)S(1)}, bf16[8,64,256]{2,1,0:T(8,128)(2,1)S(1)}, u32[]{:S(2)}, u32[]{:S(2)}) collective-permute-start(bf16[8,64,256]{2,1,0:T(8,128)(2,1)S(1)} %add_convert_fusion.2), channel_id=1, source_target_pairs={{16,0},{32,16},{48,32},{64,48},{80,64},{96,80},{112,96},{128,112},... | collective-permute-start | bytes 786440 | tf_op jit(solution)/shard_map/while/body/eval_jaxpr/ppermute | solution.py:14
  100.4 7.7 %collective-permute-start = (bf16[8,64,256]{2,1,0:T(8,128)(2,1)S(1)}, bf16[8,64,256]{2,1,0:T(8,128)(2,1)S(1)}, u32[]{:S(2)}, u32[]{:S(2)}) collective-permute-start(bf16[8,64,256]{2,1,0:T(8,128)(2,1)S(1)} %add_convert_fusion.2), channel_id=1, source_target_pairs={{16,0},{32,16},{48,32},{64,48},{80,64},{96,80},{112,96},{128,112},... | collective-permute-start | bytes 786440 | tf_op jit(solution)/shard_map/while/body/eval_jaxpr/ppermute | solution.py:14
  108.3 7.7 %collective-permute-start = (bf16[8,64,256]{2,1,0:T(8,128)(2,1)S(1)}, bf16[8,64,256]{2,1,0:T(8,128)(2,1)S(1)}, u32[]{:S(2)}, u32[]{:S(2)}) collective-permute-start(bf16[8,64,256]{2,1,0:T(8,128)(2,1)S(1)} %add_convert_fusion.2), channel_id=1, source_target_pairs={{16,0},{32,16},{48,32},{64,48},{80,64},{96,80},{112,96},{128,112},... | collective-permute-start | bytes 786440 | tf_op jit(solution)/shard_map/while/body/eval_jaxpr/ppermute | solution.py:14
  116.2 7.7 %collective-permute-start = (bf16[8,64,256]{2,1,0:T(8,128)(2,1)S(1)}, bf16[8,64,256]{2,1,0:T(8,128)(2,1)S(1)}, u32[]{:S(2)}, u32[]{:S(2)}) collective-permute-start(bf16[8,64,256]{2,1,0:T(8,128)(2,1)S(1)} %add_convert_fusion.2), channel_id=1, source_target_pairs={{16,0},{32,16},{48,32},{64,48},{80,64},{96,80},{112,96},{128,112},... | collective-permute-start | bytes 786440 | tf_op jit(solution)/shard_map/while/body/eval_jaxpr/ppermute | solution.py:14
  124.0 7.7 %collective-permute-start = (bf16[8,64,256]{2,1,0:T(8,128)(2,1)S(1)}, bf16[8,64,256]{2,1,0:T(8,128)(2,1)S(1)}, u32[]{:S(2)}, u32[]{:S(2)}) collective-permute-start(bf16[8,64,256]{2,1,0:T(8,128)(2,1)S(1)} %add_convert_fusion.2), channel_id=1, source_target_pairs={{16,0},{32,16},{48,32},{64,48},{80,64},{96,80},{112,96},{128,112},... | collective-permute-start | bytes 786440 | tf_op jit(solution)/shard_map/while/body/eval_jaxpr/ppermute | solution.py:14
  131.9 7.7 %collective-permute-start = (bf16[8,64,256]{2,1,0:T(8,128)(2,1)S(1)}, bf16[8,64,256]{2,1,0:T(8,128)(2,1)S(1)}, u32[]{:S(2)}, u32[]{:S(2)}) collective-permute-start(bf16[8,64,256]{2,1,0:T(8,128)(2,1)S(1)} %add_convert_fusion.2), channel_id=1, source_target_pairs={{16,0},{32,16},{48,32},{64,48},{80,64},{96,80},{112,96},{128,112},... | collective-permute-start | bytes 786440 | tf_op jit(solution)/shard_map/while/body/eval_jaxpr/ppermute | solution.py:14
  139.7 5.7 %copy-start.2 = (f32[4,512]{1,0:T(4,128)S(1)}, f32[4,512]{1,0:T(4,128)}, u32[]{:S(2)}) copy-start(f32[4,512]{1,0:T(4,128)} %param.19) | copy-start | bytes 24580
  143.5 4.9 %collective-permute-start.1 = (bf16[3,512]{1,0:T(4,128)(2,1)S(1)}, bf16[3,512]{1,0:T(4,128)(2,1)S(1)}, u32[]{:S(2)}, u32[]{:S(2)}) collective-permute-start(bf16[3,512]{1,0:T(4,128)(2,1)S(1)} %slice.50), channel_id=1, source_target_pairs={{16,0},{32,16},{48,32},{64,48},{80,64},{96,80},{112,96},{128,112},... | collective-permute-start | bytes 9224 | tf_op jit(solution)/shard_map/ppermute | solution.py:14
  149.8 95.2 %reduce-scatter.2.cloned.1.call-start = ((), (), s32[]{:S(2)}) async-start(), calls=%async_computation.2 | async-start | bytes 2621440 | tf_op jit(solution)/shard_map/reduce_scatter | solution.py:89
Sparse Core Ops, SparseCore 0:
  150.0 52.5 all-gather.1
  212.6 32.3 reduce-scatter.1
where the time goes:
time: 253 us; the launch traced here: 252 us
  waiting for transfers between devices  172 us (68%)
  starting transfers between devices  34 us (13%)
  matrix products  17.7 us (7%)
  between operations  14.2 us (6%)
  other arithmetic  8.98 us (4%)
  local copies, waits for them, and re-layouts  4.6 us (2%)
    ppermute x16, waiting for transfers between devices, from_behind(): lax.ppermute(value, axis, [(source, source + steps) for source in range(f...  87.5 us
    all_gather x1, waiting for transfers between devices, on_device(): lax.all_gather(x_grad, 'col', axis=1, tiled=True)  52.7 us
    ppermute x16, starting transfers between devices, from_behind(): lax.ppermute(value, axis, [(source, source + steps) for source in range(f...  34 us
    reduce_scatter x1, waiting for transfers between devices, on_device(): lax.psum_scatter(partial_grad.astype(jnp.bfloat16), 'row', scatter_dimens...  31.6 us
    dot_general x1, matrix products, on_device(): lax.dot_general(lax.all_gather(x_grad, 'col', axis=1, tiled=True), proj_w...  9.85 us
  transfers between devices with their start and end apart: 18, of which 18 were waited for; matrix products, arithmetic and copies ran while one was open for 0% of the time, Pallas kernels for 0%

commit v1 on v0

--- a/solution.py
+++ b/solution.py
@@ -81,7 +81,9 @@
         accum = accum + conv_weight[tap][None, :] * extended[tap : tap + tokens_dev]
     x_grad = accum.astype(jnp.bfloat16)
     partial_grad = lax.dot_general(
-        lax.all_gather(x_grad, "col", axis=1, tiled=True),
+        jnp.concatenate(
+            lax.all_to_all(jnp.stack([x_grad] * lax.axis_size("col")), "col", 0, 0), axis=1
+        ),
         proj_weight,
         (((1,), (1,)), ((), ())),
         preferred_element_type=jnp.float32,

time: 253 us -> 244 us (0.964)
  waiting for transfers between devices: 172 us -> 135 us
  blocking collectives: 0 us -> 29.3 us
    all_gather x1 -> x0, waiting for transfers between devices: 52.7 us -> none  [on_device(): lax.all_gather(x_grad, 'col', axis=1, tiled=True)]
    all_to_all x0 -> x1, blocking collectives: none -> 29.3 us  [on_device(): lax.all_to_all(jnp.stack([x_grad] * lax.axis_size('col')), 'col', 0, 0)]
    reduce_scatter x1, waiting for transfers between devices: 31.6 us -> 47.7 us  [on_device(): lax.psum_scatter(partial_grad.astype(jnp.bfloat16), 'row', scatter_dimens...]
  transfers between devices with their start and end apart: 18 -> 17, of which waited for: 18 -> 17; matrix products, arithmetic and copies ran while one was open for 0% -> 0% of each run, Pallas kernels for 0% -> 0%
where the time goes in v1:
time: 244 us
  waiting for transfers between devices  135 us (55%)
  starting transfers between devices  34 us (14%)
  blocking collectives  29.3 us (12%)
  matrix products  17.2 us (7%)
  between operations  14.2 us (6%)
  other arithmetic  8.18 us (3%)
  local copies, waits for them, and re-layouts  4.98 us (2%)
    ppermute x16, waiting for transfers between devices, from_behind(): lax.ppermute(value, axis, [(source, source + steps) for source in range(f...  87.5 us
    reduce_scatter x1, waiting for transfers between devices, on_device(): lax.psum_scatter(partial_grad.astype(jnp.bfloat16), 'row', scatter_dimens...  47.7 us
    ppermute x16, starting transfers between devices, from_behind(): lax.ppermute(value, axis, [(source, source + steps) for source in range(f...  34 us
    all_to_all x1, blocking collectives, on_device(): lax.all_to_all(jnp.stack([x_grad] * lax.axis_size('col')), 'col', 0, 0)  29.3 us
    dot_general x1, matrix products, on_device(): lax.dot_general(jnp.concatenate(lax.all_to_all(jnp.stack([x_grad] * lax.a...  9.34 us
  transfers between devices with their start and end apart: 17, of which 17 were waited for; matrix products, arithmetic and copies ran while one was open for 0% of the time, Pallas kernels for 0%

profile of v1, /device:TPU:1, one launch (start us, length us, event | category | flops | bytes accessed | tf_op | source)
XLA Modules:
  0.0 243.6 jit_solution(11539175523707514088)
XLA Ops:
  7.2 2.3 reduce-window.6
  11.5 2.6 %constant_dynamic-slice_fusion = (bf16[512,1,256]{2,1,0:T(2,128)(2,1)S(1)}, bf16[512,1,256]{2,1,0:T(2,128)(2,1)S(1)}) fusion(bf16[512,4,256]{2,1,0:T(4,128)(2,1)} %param.15, s32[]{:T(128)S(6)} %select_n.30, bf16[512,4,256]{2,1,0:T(4,128)(2,1)} %param.14), kind=kLoop, calls=%fused_computation.48 | loop fusion | bytes 1048580 | tf_op jit(solution)/shard_map/jit(dynamic_index_in_dim)/dynamic_slice | solution.py:34
  15.8 4.3 %fusion.2 = f32[512,8,64]{0,2,1:T(8,128)} fusion(bf16[512,8,64]{0,2,1:T(8,128)(2,1)S(1)} %bitcast.44, f32[512,512]{1,0:T(8,128)} %fusion.20, f32[8,512]{1,0:T(8,128)S(1)} %get-tuple-element.49, pred[512,512]{1,0:T(8,128)(4,1)S(1)} %iota_compare_fusion), kind=kOutput, calls=%fused_computation.6 | convolution fusion | flops 276824064 | bytes 2899968 | tf_op jit(solution)/shard_map/hts,shd->thd/dot_general | solution.py:65
  20.1 119.6 %while.10 = (s32[]{:T(128)}, f32[8,64,256]{2,1,0:T(8,128)S(1)}, pred[]{:T(512)}, f32[8]{0:T(128)S(1)}, f32[8,64,256]{2,1,0:T(8,128)S(1)}, /*index=5*/f32[8,64,256]{2,1,0:T(8,128)S(1)}, s32[]{:T(128)}) while((s32[]{:T(128)}, f32[8,64,256]{2,1,0:T(8,128)S(1)}, pred[]{:T(512)}, f32[8]{0:T(128)S(1)}, f32[8,64,256]{2,1,0:T(8,128)S(1)}, ...), condition=%wide.region_3.4_spmd, body=%wide.region_2.3_spmd.sunk | while | flops 655362 | bytes 3670166 | solution.py:51
  20.2 5.2 %collective-permute-start = (bf16[8,64,256]{2,1,0:T(8,128)(2,1)S(1)}, bf16[8,64,256]{2,1,0:T(8,128)(2,1)S(1)}, u32[]{:S(2)}, u32[]{:S(2)}) collective-permute-start(bf16[8,64,256]{2,1,0:T(8,128)(2,1)S(1)} %add_convert_fusion.2), channel_id=1, source_target_pairs={{16,0},{32,16},{48,32},{64,48},{80,64},{96,80},{112,96},{128,112},... | collective-permute-start | bytes 786440 | tf_op jit(solution)/shard_map/while/body/eval_jaxpr/ppermute | solution.py:14
  25.4 3.8 %collective-permute-done = bf16[8,64,256]{2,1,0:T(8,128)(2,1)S(1)} collective-permute-done((bf16[8,64,256]{2,1,0:T(8,128)(2,1)S(1)}, bf16[8,64,256]{2,1,0:T(8,128)(2,1)S(1)}, u32[]{:S(2)}, u32[]{:S(2)}) %collective-permute-start) | collective-permute-done | bytes 262176 | tf_op jit(solution)/shard_map/while/body/eval_jaxpr/ppermute | solution.py:14
  29.4 1.9 collective-permute-start
  31.3 5.8 %collective-permute-done = bf16[8,64,256]{2,1,0:T(8,128)(2,1)S(1)} collective-permute-done((bf16[8,64,256]{2,1,0:T(8,128)(2,1)S(1)}, bf16[8,64,256]{2,1,0:T(8,128)(2,1)S(1)}, u32[]{:S(2)}, u32[]{:S(2)}) %collective-permute-start) | collective-permute-done | bytes 262176 | tf_op jit(solution)/shard_map/while/body/eval_jaxpr/ppermute | solution.py:14
  37.3 1.9 collective-permute-start
  39.2 5.8 %collective-permute-done = bf16[8,64,256]{2,1,0:T(8,128)(2,1)S(1)} collective-permute-done((bf16[8,64,256]{2,1,0:T(8,128)(2,1)S(1)}, bf16[8,64,256]{2,1,0:T(8,128)(2,1)S(1)}, u32[]{:S(2)}, u32[]{:S(2)}) %collective-permute-start) | collective-permute-done | bytes 262176 | tf_op jit(solution)/shard_map/while/body/eval_jaxpr/ppermute | solution.py:14
  45.2 1.9 collective-permute-start
  47.1 5.8 %collective-permute-done = bf16[8,64,256]{2,1,0:T(8,128)(2,1)S(1)} collective-permute-done((bf16[8,64,256]{2,1,0:T(8,128)(2,1)S(1)}, bf16[8,64,256]{2,1,0:T(8,128)(2,1)S(1)}, u32[]{:S(2)}, u32[]{:S(2)}) %collective-permute-start) | collective-permute-done | bytes 262176 | tf_op jit(solution)/shard_map/while/body/eval_jaxpr/ppermute | solution.py:14
  55.0 5.8 %collective-permute-done = bf16[8,64,256]{2,1,0:T(8,128)(2,1)S(1)} collective-permute-done((bf16[8,64,256]{2,1,0:T(8,128)(2,1)S(1)}, bf16[8,64,256]{2,1,0:T(8,128)(2,1)S(1)}, u32[]{:S(2)}, u32[]{:S(2)}) %collective-permute-start) | collective-permute-done | bytes 262176 | tf_op jit(solution)/shard_map/while/body/eval_jaxpr/ppermute | solution.py:14
  62.9 5.8 %collective-permute-done = bf16[8,64,256]{2,1,0:T(8,128)(2,1)S(1)} collective-permute-done((bf16[8,64,256]{2,1,0:T(8,128)(2,1)S(1)}, bf16[8,64,256]{2,1,0:T(8,128)(2,1)S(1)}, u32[]{:S(2)}, u32[]{:S(2)}) %collective-permute-start) | collective-permute-done | bytes 262176 | tf_op jit(solution)/shard_map/while/body/eval_jaxpr/ppermute | solution.py:14
  70.8 5.8 %collective-permute-done = bf16[8,64,256]{2,1,0:T(8,128)(2,1)S(1)} collective-permute-done((bf16[8,64,256]{2,1,0:T(8,128)(2,1)S(1)}, bf16[8,64,256]{2,1,0:T(8,128)(2,1)S(1)}, u32[]{:S(2)}, u32[]{:S(2)}) %collective-permute-start) | collective-permute-done | bytes 262176 | tf_op jit(solution)/shard_map/while/body/eval_jaxpr/ppermute | solution.py:14
  76.7 1.9 collective-permute-start
  78.7 5.8 %collective-permute-done = bf16[8,64,256]{2,1,0:T(8,128)(2,1)S(1)} collective-permute-done((bf16[8,64,256]{2,1,0:T(8,128)(2,1)S(1)}, bf16[8,64,256]{2,1,0:T(8,128)(2,1)S(1)}, u32[]{:S(2)}, u32[]{:S(2)}) %collective-permute-start) | collective-permute-done | bytes 262176 | tf_op jit(solution)/shard_map/while/body/eval_jaxpr/ppermute | solution.py:14
  84.6 1.9 collective-permute-start
  86.5 5.8 %collective-permute-done = bf16[8,64,256]{2,1,0:T(8,128)(2,1)S(1)} collective-permute-done((bf16[8,64,256]{2,1,0:T(8,128)(2,1)S(1)}, bf16[8,64,256]{2,1,0:T(8,128)(2,1)S(1)}, u32[]{:S(2)}, u32[]{:S(2)}) %collective-permute-start) | collective-permute-done | bytes 262176 | tf_op jit(solution)/shard_map/while/body/eval_jaxpr/ppermute | solution.py:14
  92.5 1.9 collective-permute-start
  94.4 5.8 %collective-permute-done = bf16[8,64,256]{2,1,0:T(8,128)(2,1)S(1)} collective-permute-done((bf16[8,64,256]{2,1,0:T(8,128)(2,1)S(1)}, bf16[8,64,256]{2,1,0:T(8,128)(2,1)S(1)}, u32[]{:S(2)}, u32[]{:S(2)}) %collective-permute-start) | collective-permute-done | bytes 262176 | tf_op jit(solution)/shard_map/while/body/eval_jaxpr/ppermute | solution.py:14
  102.3 5.8 %collective-permute-done = bf16[8,64,256]{2,1,0:T(8,128)(2,1)S(1)} collective-permute-done((bf16[8,64,256]{2,1,0:T(8,128)(2,1)S(1)}, bf16[8,64,256]{2,1,0:T(8,128)(2,1)S(1)}, u32[]{:S(2)}, u32[]{:S(2)}) %collective-permute-start) | collective-permute-done | bytes 262176 | tf_op jit(solution)/shard_map/while/body/eval_jaxpr/ppermute | solution.py:14
  110.2 5.8 %collective-permute-done = bf16[8,64,256]{2,1,0:T(8,128)(2,1)S(1)} collective-permute-done((bf16[8,64,256]{2,1,0:T(8,128)(2,1)S(1)}, bf16[8,64,256]{2,1,0:T(8,128)(2,1)S(1)}, u32[]{:S(2)}, u32[]{:S(2)}) %collective-permute-start) | collective-permute-done | bytes 262176 | tf_op jit(solution)/shard_map/while/body/eval_jaxpr/ppermute | solution.py:14
  118.1 5.8 %collective-permute-done = bf16[8,64,256]{2,1,0:T(8,128)(2,1)S(1)} collective-permute-done((bf16[8,64,256]{2,1,0:T(8,128)(2,1)S(1)}, bf16[8,64,256]{2,1,0:T(8,128)(2,1)S(1)}, u32[]{:S(2)}, u32[]{:S(2)}) %collective-permute-start) | collective-permute-done | bytes 262176 | tf_op jit(solution)/shard_map/while/body/eval_jaxpr/ppermute | solution.py:14
  126.0 5.8 %collective-permute-done = bf16[8,64,256]{2,1,0:T(8,128)(2,1)S(1)} collective-permute-done((bf16[8,64,256]{2,1,0:T(8,128)(2,1)S(1)}, bf16[8,64,256]{2,1,0:T(8,128)(2,1)S(1)}, u32[]{:S(2)}, u32[]{:S(2)}) %collective-permute-start) | collective-permute-done | bytes 262176 | tf_op jit(solution)/shard_map/while/body/eval_jaxpr/ppermute | solution.py:14
  133.9 5.8 %collective-permute-done = bf16[8,64,256]{2,1,0:T(8,128)(2,1)S(1)} collective-permute-done((bf16[8,64,256]{2,1,0:T(8,128)(2,1)S(1)}, bf16[8,64,256]{2,1,0:T(8,128)(2,1)S(1)}, u32[]{:S(2)}, u32[]{:S(2)}) %collective-permute-start) | collective-permute-done | bytes 262176 | tf_op jit(solution)/shard_map/while/body/eval_jaxpr/ppermute | solution.py:14
  139.7 2.0 fusion.5
  143.5 1.9 collective-permute-start.1
  145.5 3.0 %collective-permute-done.1 = bf16[3,512]{1,0:T(4,128)(2,1)S(1)} collective-permute-done((bf16[3,512]{1,0:T(4,128)(2,1)S(1)}, bf16[3,512]{1,0:T(4,128)(2,1)S(1)}, u32[]{:S(2)}, u32[]{:S(2)}) %collective-permute-start.1) | collective-permute-done | bytes 3104 | tf_op jit(solution)/shard_map/ppermute | solution.py:14
  149.4 29.3 %all_to_all.5 = bf16[4,512,512]{1,2,0:T(8,128)(2,1)S(1)} all-to-all(bf16[4,512,512]{1,2,0:T(8,128)(2,1)S(1)} %stack.2), channel_id=1, replica_groups=mesh['ctx'=16,'row'=4,'col'=4] {'col'}, dimensions={0} | all-to-all | bytes 4194304 | tf_op jit(solution)/shard_map/all_to_all | solution.py:85
  178.7 9.3 %convolution_convert_fusion = bf16[512,2048]{1,0:T(8,128)(2,1)} fusion(bf16[512,2048]{0,1:T(8,128)(2,1)S(1)} %bitcast.47, bf16[2048,2048]{1,0:T(8,128)(2,1)} %param.21), kind=kOutput, calls=%fused_computation.5 | convolution fusion | flops 4296015872 | bytes 12582912 | tf_op jit(solution)/shard_map/dot_general | solution.py:83
  189.0 47.7 %reduce-scatter.2.cloned.1.call-done = bf16[512,512]{1,0:T(8,128)(2,1)} async-done(((bf16[512,2048]{1,0:T(8,128)(2,1)}), bf16[512,512]{1,0:T(8,128)(2,1)}) %reduce-scatter.2.cloned.1.call-update) | async-done | bytes 524304 | tf_op jit(solution)/shard_map/reduce_scatter | solution.py:91
  (72 shorter events, 25.3 us)
Async XLA Ops:
  7.2 8.6 %copy-start = (f32[8,64,256]{2,1,0:T(8,128)S(1)}, f32[8,64,256]{2,1,0:T(8,128)}, u32[]{:S(2)}) copy-start(f32[8,64,256]{2,1,0:T(8,128)} %param.20) | copy-start | bytes 1572868
  7.2 229.6 %reduce-scatter.2.cloned.1.call-start = ((), (), s32[]{:S(2)}) async-start(), calls=%async_computation.2 | async-start | bytes 2621440 | tf_op jit(solution)/shard_map/reduce_scatter | solution.py:91
  20.1 119.6 %copy-start.2 = (f32[8,512]{1,0:T(8,128)S(1)}, f32[8,512]{1,0:T(8,128)}, u32[]{:S(2)}) copy-start(f32[8,512]{1,0:T(8,128)} %param.16) | copy-start | bytes 49156
  20.1 119.6 %copy-start.4 = (f32[8]{0:T(128)S(1)}, f32[8]{0:T(128)}, u32[]{:S(2)}) copy-start(f32[8]{0:T(128)} %param.18) | copy-start | bytes 100
  20.2 9.0 %collective-permute-start = (bf16[8,64,256]{2,1,0:T(8,128)(2,1)S(1)}, bf16[8,64,256]{2,1,0:T(8,128)(2,1)S(1)}, u32[]{:S(2)}, u32[]{:S(2)}) collective-permute-start(bf16[8,64,256]{2,1,0:T(8,128)(2,1)S(1)} %add_convert_fusion.2), channel_id=1, source_target_pairs={{16,0},{32,16},{48,32},{64,48},{80,64},{96,80},{112,96},{128,112},... | collective-permute-start | bytes 786440 | tf_op jit(solution)/shard_map/while/body/eval_jaxpr/ppermute | solution.py:14
  29.4 7.7 %collective-permute-start = (bf16[8,64,256]{2,1,0:T(8,128)(2,1)S(1)}, bf16[8,64,256]{2,1,0:T(8,128)(2,1)S(1)}, u32[]{:S(2)}, u32[]{:S(2)}) collective-permute-start(bf16[8,64,256]{2,1,0:T(8,128)(2,1)S(1)} %add_convert_fusion.2), channel_id=1, source_target_pairs={{16,0},{32,16},{48,32},{64,48},{80,64},{96,80},{112,96},{128,112},... | collective-permute-start | bytes 786440 | tf_op jit(solution)/shard_map/while/body/eval_jaxpr/ppermute | solution.py:14
  37.3 7.7 %collective-permute-start = (bf16[8,64,256]{2,1,0:T(8,128)(2,1)S(1)}, bf16[8,64,256]{2,1,0:T(8,128)(2,1)S(1)}, u32[]{:S(2)}, u32[]{:S(2)}) collective-permute-start(bf16[8,64,256]{2,1,0:T(8,128)(2,1)S(1)} %add_convert_fusion.2), channel_id=1, source_target_pairs={{16,0},{32,16},{48,32},{64,48},{80,64},{96,80},{112,96},{128,112},... | collective-permute-start | bytes 786440 | tf_op jit(solution)/shard_map/while/body/eval_jaxpr/ppermute | solution.py:14
  45.2 7.7 %collective-permute-start = (bf16[8,64,256]{2,1,0:T(8,128)(2,1)S(1)}, bf16[8,64,256]{2,1,0:T(8,128)(2,1)S(1)}, u32[]{:S(2)}, u32[]{:S(2)}) collective-permute-start(bf16[8,64,256]{2,1,0:T(8,128)(2,1)S(1)} %add_convert_fusion.2), channel_id=1, source_target_pairs={{16,0},{32,16},{48,32},{64,48},{80,64},{96,80},{112,96},{128,112},... | collective-permute-start | bytes 786440 | tf_op jit(solution)/shard_map/while/body/eval_jaxpr/ppermute | solution.py:14
  53.1 7.7 %collective-permute-start = (bf16[8,64,256]{2,1,0:T(8,128)(2,1)S(1)}, bf16[8,64,256]{2,1,0:T(8,128)(2,1)S(1)}, u32[]{:S(2)}, u32[]{:S(2)}) collective-permute-start(bf16[8,64,256]{2,1,0:T(8,128)(2,1)S(1)} %add_convert_fusion.2), channel_id=1, source_target_pairs={{16,0},{32,16},{48,32},{64,48},{80,64},{96,80},{112,96},{128,112},... | collective-permute-start | bytes 786440 | tf_op jit(solution)/shard_map/while/body/eval_jaxpr/ppermute | solution.py:14
  61.0 7.7 %collective-permute-start = (bf16[8,64,256]{2,1,0:T(8,128)(2,1)S(1)}, bf16[8,64,256]{2,1,0:T(8,128)(2,1)S(1)}, u32[]{:S(2)}, u32[]{:S(2)}) collective-permute-start(bf16[8,64,256]{2,1,0:T(8,128)(2,1)S(1)} %add_convert_fusion.2), channel_id=1, source_target_pairs={{16,0},{32,16},{48,32},{64,48},{80,64},{96,80},{112,96},{128,112},... | collective-permute-start | bytes 786440 | tf_op jit(solution)/shard_map/while/body/eval_jaxpr/ppermute | solution.py:14
  68.8 7.7 %collective-permute-start = (bf16[8,64,256]{2,1,0:T(8,128)(2,1)S(1)}, bf16[8,64,256]{2,1,0:T(8,128)(2,1)S(1)}, u32[]{:S(2)}, u32[]{:S(2)}) collective-permute-start(bf16[8,64,256]{2,1,0:T(8,128)(2,1)S(1)} %add_convert_fusion.2), channel_id=1, source_target_pairs={{16,0},{32,16},{48,32},{64,48},{80,64},{96,80},{112,96},{128,112},... | collective-permute-start | bytes 786440 | tf_op jit(solution)/shard_map/while/body/eval_jaxpr/ppermute | solution.py:14
  76.7 7.7 %collective-permute-start = (bf16[8,64,256]{2,1,0:T(8,128)(2,1)S(1)}, bf16[8,64,256]{2,1,0:T(8,128)(2,1)S(1)}, u32[]{:S(2)}, u32[]{:S(2)}) collective-permute-start(bf16[8,64,256]{2,1,0:T(8,128)(2,1)S(1)} %add_convert_fusion.2), channel_id=1, source_target_pairs={{16,0},{32,16},{48,32},{64,48},{80,64},{96,80},{112,96},{128,112},... | collective-permute-start | bytes 786440 | tf_op jit(solution)/shard_map/while/body/eval_jaxpr/ppermute | solution.py:14
  84.6 7.7 %collective-permute-start = (bf16[8,64,256]{2,1,0:T(8,128)(2,1)S(1)}, bf16[8,64,256]{2,1,0:T(8,128)(2,1)S(1)}, u32[]{:S(2)}, u32[]{:S(2)}) collective-permute-start(bf16[8,64,256]{2,1,0:T(8,128)(2,1)S(1)} %add_convert_fusion.2), channel_id=1, source_target_pairs={{16,0},{32,16},{48,32},{64,48},{80,64},{96,80},{112,96},{128,112},... | collective-permute-start | bytes 786440 | tf_op jit(solution)/shard_map/while/body/eval_jaxpr/ppermute | solution.py:14
  92.5 7.7 %collective-permute-start = (bf16[8,64,256]{2,1,0:T(8,128)(2,1)S(1)}, bf16[8,64,256]{2,1,0:T(8,128)(2,1)S(1)}, u32[]{:S(2)}, u32[]{:S(2)}) collective-permute-start(bf16[8,64,256]{2,1,0:T(8,128)(2,1)S(1)} %add_convert_fusion.2), channel_id=1, source_target_pairs={{16,0},{32,16},{48,32},{64,48},{80,64},{96,80},{112,96},{128,112},... | collective-permute-start | bytes 786440 | tf_op jit(solution)/shard_map/while/body/eval_jaxpr/ppermute | solution.py:14
  100.4 7.7 %collective-permute-start = (bf16[8,64,256]{2,1,0:T(8,128)(2,1)S(1)}, bf16[8,64,256]{2,1,0:T(8,128)(2,1)S(1)}, u32[]{:S(2)}, u32[]{:S(2)}) collective-permute-start(bf16[8,64,256]{2,1,0:T(8,128)(2,1)S(1)} %add_convert_fusion.2), channel_id=1, source_target_pairs={{16,0},{32,16},{48,32},{64,48},{80,64},{96,80},{112,96},{128,112},... | collective-permute-start | bytes 786440 | tf_op jit(solution)/shard_map/while/body/eval_jaxpr/ppermute | solution.py:14
  108.3 7.7 %collective-permute-start = (bf16[8,64,256]{2,1,0:T(8,128)(2,1)S(1)}, bf16[8,64,256]{2,1,0:T(8,128)(2,1)S(1)}, u32[]{:S(2)}, u32[]{:S(2)}) collective-permute-start(bf16[8,64,256]{2,1,0:T(8,128)(2,1)S(1)} %add_convert_fusion.2), channel_id=1, source_target_pairs={{16,0},{32,16},{48,32},{64,48},{80,64},{96,80},{112,96},{128,112},... | collective-permute-start | bytes 786440 | tf_op jit(solution)/shard_map/while/body/eval_jaxpr/ppermute | solution.py:14
  116.2 7.7 %collective-permute-start = (bf16[8,64,256]{2,1,0:T(8,128)(2,1)S(1)}, bf16[8,64,256]{2,1,0:T(8,128)(2,1)S(1)}, u32[]{:S(2)}, u32[]{:S(2)}) collective-permute-start(bf16[8,64,256]{2,1,0:T(8,128)(2,1)S(1)} %add_convert_fusion.2), channel_id=1, source_target_pairs={{16,0},{32,16},{48,32},{64,48},{80,64},{96,80},{112,96},{128,112},... | collective-permute-start | bytes 786440 | tf_op jit(solution)/shard_map/while/body/eval_jaxpr/ppermute | solution.py:14
  124.1 7.7 %collective-permute-start = (bf16[8,64,256]{2,1,0:T(8,128)(2,1)S(1)}, bf16[8,64,256]{2,1,0:T(8,128)(2,1)S(1)}, u32[]{:S(2)}, u32[]{:S(2)}) collective-permute-start(bf16[8,64,256]{2,1,0:T(8,128)(2,1)S(1)} %add_convert_fusion.2), channel_id=1, source_target_pairs={{16,0},{32,16},{48,32},{64,48},{80,64},{96,80},{112,96},{128,112},... | collective-permute-start | bytes 786440 | tf_op jit(solution)/shard_map/while/body/eval_jaxpr/ppermute | solution.py:14
  131.9 7.7 %collective-permute-start = (bf16[8,64,256]{2,1,0:T(8,128)(2,1)S(1)}, bf16[8,64,256]{2,1,0:T(8,128)(2,1)S(1)}, u32[]{:S(2)}, u32[]{:S(2)}) collective-permute-start(bf16[8,64,256]{2,1,0:T(8,128)(2,1)S(1)} %add_convert_fusion.2), channel_id=1, source_target_pairs={{16,0},{32,16},{48,32},{64,48},{80,64},{96,80},{112,96},{128,112},... | collective-permute-start | bytes 786440 | tf_op jit(solution)/shard_map/while/body/eval_jaxpr/ppermute | solution.py:14
  139.7 5.7 %copy-start.3 = (f32[4,512]{1,0:T(4,128)S(1)}, f32[4,512]{1,0:T(4,128)}, u32[]{:S(2)}) copy-start(f32[4,512]{1,0:T(4,128)} %param.19) | copy-start | bytes 24580
  143.5 4.9 %collective-permute-start.1 = (bf16[3,512]{1,0:T(4,128)(2,1)S(1)}, bf16[3,512]{1,0:T(4,128)(2,1)S(1)}, u32[]{:S(2)}, u32[]{:S(2)}) collective-permute-start(bf16[3,512]{1,0:T(4,128)(2,1)S(1)} %slice.50), channel_id=1, source_target_pairs={{16,0},{32,16},{48,32},{64,48},{80,64},{96,80},{112,96},{128,112},... | collective-permute-start | bytes 9224 | tf_op jit(solution)/shard_map/ppermute | solution.py:14
  149.0 39.0 %copy-start.1 = (bf16[512,512]{1,0:T(8,128)(2,1)}, bf16[512,512]{1,0:T(8,128)(2,1)S(1)}, u32[]{:S(2)}) copy-start(bf16[512,512]{1,0:T(8,128)(2,1)S(1)} %fusion.13) | copy-start | bytes 1572868
Sparse Core Ops, SparseCore 0:
  188.2 48.4 reduce-scatter.1
